TPU v7x, 32 devices: a whole 2x2x4 slice. The times are simulated.
32 devices in a mesh: dp: 8 (over z, x), mp: 4 (over y, core).
Axes of the slice: x: 2, y: 2, z: 4, core: 2. Of those that a mesh axis runs over, the one named last changes fastest.
Arguments:
- tokens: bfloat16 [32768, 1024], P('dp'), may hold values from -12 to 12
- out_grad: bfloat16 [32768, 1024], P('dp'), may hold values from -12 to 12
- qk_weight: float32 [2, 1024, 256], P(None, 'dp'), may hold values from -0.1875 to 0.1875
- qk_first: float32 [2, 1024, 256], P(None, 'dp'), may hold values from -0.0048828125 to 0.0048828125
- qk_second: float32 [2, 1024, 256], P(None, 'dp'), may hold values from 5.839972e-07 to 2.3359887e-06
- qk_average: float32 [2, 1024, 256], P(None, 'dp'), may hold values from -0.1875 to 0.1875
- value_weight: float32 [1024, 1024], P('dp', 'mp'), may hold values from -0.1875 to 0.1875
- value_first: float32 [1024, 1024], P('dp', 'mp'), may hold values from -0.0024414062 to 0.0024414062
- value_second: float32 [1024, 1024], P('dp', 'mp'), may hold values from 1.9069296e-07 to 7.6277183e-07
- value_average: float32 [1024, 1024], P('dp', 'mp'), may hold values from -0.1875 to 0.1875
- output_weight: float32 [1024, 1024], P('mp', 'dp'), may hold values from -1.5 to 1.5
- output_first: float32 [1024, 1024], P('mp', 'dp'), may hold values from -0.00048828125 to 0.00048828125
- output_second: float32 [1024, 1024], P('mp', 'dp'), may hold values from 6.7040493e-09 to 2.6816197e-08
- output_average: float32 [1024, 1024], P('mp', 'dp'), may hold values from -1.5 to 1.5
- gate_up_weight: float32 [2, 1024, 2752], P(None, 'dp', 'mp'), may hold values from -0.1875 to 0.1875
- gate_up_first: float32 [2, 1024, 2752], P(None, 'dp', 'mp'), may hold values from -0.0009765625 to 0.0009765625
- gate_up_second: float32 [2, 1024, 2752], P(None, 'dp', 'mp'), may hold values from 3.2775354e-08 to 1.3110142e-07
- gate_up_average: float32 [2, 1024, 2752], P(None, 'dp', 'mp'), may hold values from -0.1875 to 0.1875
- down_weight: float32 [2752, 1024], P('mp', 'dp'), may hold values from -0.109375 to 0.109375
- down_first: float32 [2752, 1024], P('mp', 'dp'), may hold values from -0.001953125 to 0.001953125
- down_second: float32 [2752, 1024], P('mp', 'dp'), may hold values from 1.0726479e-07 to 4.2905916e-07
- down_average: float32 [2752, 1024], P('mp', 'dp'), may hold values from -0.109375 to 0.109375
- gains: float32 [2, 1024], P(None, 'dp'), may hold values from 0.5 to 1.5
- gains_first: float32 [2, 1024], P(None, 'dp'), may hold values from -0.0034179688 to 0.0034179688
- gains_second: float32 [2, 1024], P(None, 'dp'), may hold values from 2.9795777e-07 to 1.1918311e-06
- gains_average: float32 [2, 1024], P(None, 'dp'), may hold values from 0.5 to 1.5
Outputs:
- block_out: bfloat16 [32768, 1024], P('dp', 'mp')
- input_grad: float32 [32768, 1024], P('dp', 'mp')
- grad_norm: float32 [], replicated
- qk_first_new: float32 [2, 1024, 256], P(None, 'dp')
- qk_second_new: float32 [2, 1024, 256], P(None, 'dp')
- qk_new: float32 [2, 1024, 256], P(None, 'dp')
- qk_average_new: float32 [2, 1024, 256], P(None, 'dp')
- value_first_new: float32 [1024, 1024], P('dp', 'mp')
- value_second_new: float32 [1024, 1024], P('dp', 'mp')
- value_new: float32 [1024, 1024], P('dp', 'mp')
- value_average_new: float32 [1024, 1024], P('dp', 'mp')
- output_first_new: float32 [1024, 1024], P('mp', 'dp')
- output_second_new: float32 [1024, 1024], P('mp', 'dp')
- output_new: float32 [1024, 1024], P('mp', 'dp')
- output_average_new: float32 [1024, 1024], P('mp', 'dp')
- gate_up_first_new: float32 [2, 1024, 2752], P(None, 'dp', 'mp')
- gate_up_second_new: float32 [2, 1024, 2752], P(None, 'dp', 'mp')
- gate_up_new: float32 [2, 1024, 2752], P(None, 'dp', 'mp')
- gate_up_average_new: float32 [2, 1024, 2752], P(None, 'dp', 'mp')
- down_first_new: float32 [2752, 1024], P('mp', 'dp')
- down_second_new: float32 [2752, 1024], P('mp', 'dp')
- down_new: float32 [2752, 1024], P('mp', 'dp')
- down_average_new: float32 [2752, 1024], P('mp', 'dp')
- gains_first_new: float32 [2, 1024], P(None, 'dp')
- gains_second_new: float32 [2, 1024], P(None, 'dp')
- gains_new: float32 [2, 1024], P(None, 'dp')
- gains_average_new: float32 [2, 1024], P(None, 'dp')
All inputs are finite; a program needn't handle non-finite values.
Results may differ from a plain program's by a relative error of at most 0.018.
Values may be sent and summed in bfloat16 or wider, within the bound.
A program may use at most 256 MiB of HBM per device.

v0:
```python
import math
import jax
import jax.numpy as jnp
from jax import lax
from jax.sharding import PartitionSpec as P

D = 1024
H = 16
F = 16
VH = 64
FF = 2752
V_ALL = 1024
LEN = 1024
STEP = 5


def inner(left, right):
    return lax.dot_general(
        left, right, (((0,), (0,)), ((), ())), preferred_element_type=jnp.float32
    )


def against(left, right):
    return lax.dot_general(
        left, right, (((1,), (1,)), ((), ())), preferred_element_type=jnp.float32
    )


def rms_scale(values):
    return lax.rsqrt(jnp.mean(values * values, axis=1, keepdims=True) + 1e-05)


def score_table(query, keys):
    length = query.shape[0]
    causal = (jnp.arange(length)[:, None] >= jnp.arange(length)[None, :]).astype(jnp.float32)
    tiled = jnp.einsum("ihf,jhf->hij", query, keys, preferred_element_type=jnp.float32) / math.sqrt(
        query.shape[2]
    )
    return (tiled, causal)


def mix_forward(parts):
    query, keys, values = parts
    tiled, causal = score_table(query, keys)
    kernel = causal * (1.0 + tiled + 0.5 * tiled * tiled)
    numer = jnp.einsum(
        "hij,jhv->ihv", kernel.astype(jnp.bfloat16), values, preferred_element_type=jnp.float32
    )
    return (numer, jnp.sum(kernel, axis=2).T)


def mix_backward(parts):
    query, keys, values, numer, denom, grad_mixed = parts
    tiled, causal = score_table(query, keys)
    kernel = causal * (1.0 + tiled + 0.5 * tiled * tiled)
    grad_numer = (grad_mixed / denom[:, :, None]).astype(jnp.bfloat16)
    grad_denom = -jnp.sum(grad_mixed * numer, axis=2) / (denom * denom)
    grad_kernel = (
        jnp.einsum("ihv,jhv->hij", grad_numer, values, preferred_element_type=jnp.float32)
        + grad_denom.T[:, :, None]
    )
    grad_tiled = (causal * grad_kernel * (1.0 + tiled)).astype(jnp.bfloat16)
    root = math.sqrt(query.shape[2])
    grad_values = jnp.einsum(
        "hij,ihv->jhv", kernel.astype(jnp.bfloat16), grad_numer, preferred_element_type=jnp.float32
    ).astype(jnp.bfloat16)
    grad_query = (
        jnp.einsum("hij,jhf->ihf", grad_tiled, keys, preferred_element_type=jnp.float32) / root
    ).astype(jnp.bfloat16)
    grad_keys = (
        jnp.einsum("hij,ihf->jhf", grad_tiled, query, preferred_element_type=jnp.float32) / root
    ).astype(jnp.bfloat16)
    return (grad_query, grad_keys, grad_values)


def adam_step(grad, first, second, weight, average, rate):
    first = 0.5 * first + 0.5 * grad
    second = 0.5 * second + 0.5 * grad * grad
    correct = 1.0 - 0.5**STEP
    weight = weight - rate * (first / correct / (jnp.sqrt(second / correct) + 1e-08) + 0.1 * weight)
    average = 0.5 * average + 0.5 * weight
    return (first, second, weight, average)


def on_device(
    tokens,
    out_grad,
    qk_weight,
    qk_first,
    qk_second,
    qk_average,
    value_weight,
    value_first,
    value_second,
    value_average,
    output_weight,
    output_first,
    output_second,
    output_average,
    gate_up_weight,
    gate_up_first,
    gate_up_second,
    gate_up_average,
    down_weight,
    down_first,
    down_second,
    down_average,
    gains,
    gains_first,
    gains_second,
    gains_average,
):
    groups = lax.axis_size("mp")
    rank = lax.axis_index("mp")
    qk_full, value_local, output_local, gate_up_local, down_local, gains_full = (
        lax.all_gather(qk_weight.astype(jnp.bfloat16), "dp", axis=1, tiled=True),
        lax.all_gather(value_weight.astype(jnp.bfloat16), "dp", axis=0, tiled=True),
        lax.all_gather(output_weight.astype(jnp.bfloat16), "dp", axis=1, tiled=True),
        lax.all_gather(gate_up_weight.astype(jnp.bfloat16), "dp", axis=1, tiled=True),
        lax.all_gather(down_weight.astype(jnp.bfloat16), "dp", axis=1, tiled=True),
        lax.all_gather(gains.astype(jnp.bfloat16), "dp", axis=1, tiled=True),
    )
    width = qk_full.shape[2] // groups
    qk_local = lax.dynamic_slice_in_dim(qk_full, rank * width, width, 2)
    tok_count = tokens.shape[0]
    seq_count = tok_count // LEN
    heads_here = H // groups
    cols = tokens.shape[1] // groups
    col_start = rank * cols
    first_gain = gains_full[0].astype(jnp.float32)
    second_gain = gains_full[1].astype(jnp.float32)
    inputs = tokens.astype(jnp.float32)
    scale_one = rms_scale(inputs)
    normed_one = inputs * scale_one
    hidden_one = (normed_one * first_gain).astype(jnp.bfloat16)
    query = jnp.dot(hidden_one, qk_local[0], preferred_element_type=jnp.float32).astype(
        jnp.bfloat16
    )
    keys = jnp.dot(hidden_one, qk_local[1], preferred_element_type=jnp.float32).astype(jnp.bfloat16)
    values = jnp.dot(hidden_one, value_local, preferred_element_type=jnp.float32).astype(
        jnp.bfloat16
    )
    head_query = query.reshape(seq_count, LEN, heads_here, F)
    head_keys = keys.reshape(seq_count, LEN, heads_here, F)
    head_values = values.reshape(seq_count, LEN, heads_here, VH)
    numer, denom = lax.map(mix_forward, (head_query, head_keys, head_values))
    mixed = (numer / denom[:, :, :, None]).astype(jnp.bfloat16).reshape(tok_count, heads_here * VH)
    attn_part = jnp.dot(mixed, output_local, preferred_element_type=jnp.float32)
    resid = inputs + lax.psum(attn_part.astype(jnp.bfloat16), "mp").astype(jnp.float32)
    scale_two = rms_scale(resid)
    normed_two = resid * scale_two
    hidden_two = (normed_two * second_gain).astype(jnp.bfloat16)
    gate = jnp.dot(hidden_two, gate_up_local[0], preferred_element_type=jnp.float32)
    lift = jnp.dot(hidden_two, gate_up_local[1], preferred_element_type=jnp.float32)
    sigma = jax.nn.sigmoid(gate)
    activ = (gate * sigma * lift).astype(jnp.bfloat16)
    down_part = jnp.dot(activ, down_local, preferred_element_type=jnp.float32)
    block_out = (
        lax.dynamic_slice_in_dim(resid, col_start, cols, 1)
        + lax.psum_scatter(
            down_part.astype(jnp.bfloat16), "mp", scatter_dimension=1, tiled=True
        ).astype(jnp.float32)
    ).astype(jnp.bfloat16)
    cotan = out_grad.astype(jnp.float32)
    grad_activ = against(out_grad, down_local)
    down_grad = inner(activ, out_grad)
    grad_gate = (grad_activ * lift * sigma * (1.0 + gate * (1.0 - sigma))).astype(jnp.bfloat16)
    grad_lift = (grad_activ * gate * sigma).astype(jnp.bfloat16)
    gate_up_grad = jnp.stack((inner(hidden_two, grad_gate), inner(hidden_two, grad_lift)))
    back_two = lax.psum(
        (against(grad_gate, gate_up_local[0]) + against(grad_lift, gate_up_local[1])).astype(
            jnp.bfloat16
        ),
        "mp",
    ).astype(jnp.float32)
    gain_two = jnp.sum(back_two * normed_two, axis=0)
    grad_resid = (
        cotan
        + scale_two * second_gain * back_two
        - resid * scale_two**3 * jnp.mean(resid * second_gain * back_two, axis=1, keepdims=True)
    )
    resid_low = grad_resid.astype(jnp.bfloat16)
    output_grad = inner(mixed, resid_low)
    grad_mixed = against(resid_low, output_local).reshape(seq_count, LEN, heads_here, VH)
    grad_query, grad_keys, grad_values = lax.map(
        mix_backward, (head_query, head_keys, head_values, numer, denom, grad_mixed)
    )
    grad_query = grad_query.reshape(tok_count, width)
    grad_keys = grad_keys.reshape(tok_count, width)
    grad_values = grad_values.reshape(tok_count, heads_here * VH)
    qk_grad = jnp.stack((inner(hidden_one, grad_query), inner(hidden_one, grad_keys)))
    value_grad = inner(hidden_one, grad_values)
    back_one = (
        against(grad_query, qk_local[0])
        + against(grad_keys, qk_local[1])
        + against(grad_values, value_local)
    )
    input_part = scale_one * first_gain * back_one - inputs * scale_one**3 * jnp.mean(
        inputs * first_gain * back_one, axis=1, keepdims=True
    )
    gains_grad = jnp.stack((jnp.sum(back_one * normed_one, axis=0), gain_two))
    input_grad = lax.dynamic_slice_in_dim(grad_resid, col_start, cols, 1) + lax.psum_scatter(
        input_part.astype(jnp.bfloat16), "mp", scatter_dimension=1, tiled=True
    ).astype(jnp.float32)
    qk_grad = lax.all_gather(qk_grad.astype(jnp.bfloat16), "mp", axis=2, tiled=True).astype(
        qk_grad.dtype
    )
    qk_share, value_share, output_share, gate_up_share, down_share, gains_share = (
        lax.psum_scatter(qk_grad, "dp", scatter_dimension=1, tiled=True),
        lax.psum_scatter(value_grad, "dp", scatter_dimension=0, tiled=True),
        lax.psum_scatter(output_grad, "dp", scatter_dimension=1, tiled=True),
        lax.psum_scatter(gate_up_grad, "dp", scatter_dimension=1, tiled=True),
        lax.psum_scatter(down_grad, "dp", scatter_dimension=1, tiled=True),
        lax.psum_scatter(gains_grad, "dp", scatter_dimension=1, tiled=True),
    )
    first_row = lax.psum(gains_share[0], "mp")
    gains_share = jnp.stack((first_row, gains_share[1]))
    spread_sum = (
        jnp.sum(value_share * value_share)
        + jnp.sum(output_share * output_share)
        + jnp.sum(gate_up_share * gate_up_share)
        + jnp.sum(down_share * down_share)
    )
    shared_sum = jnp.sum(qk_share * qk_share) + jnp.sum(gains_share * gains_share)
    total = lax.psum(spread_sum + shared_sum / groups, ("dp", "mp"))
    grad_norm = jnp.sqrt(total)
    clip = jnp.minimum(1.0, 1.0 / (grad_norm + 1e-06))
    qk_m, qk_v, qk_w, qk_a = adam_step(
        clip * qk_share, qk_first, qk_second, qk_weight, qk_average, 1.0 / math.sqrt(D)
    )
    value_m, value_v, value_w, value_a = adam_step(
        clip * value_share,
        value_first,
        value_second,
        value_weight,
        value_average,
        1.0 / math.sqrt(D),
    )
    output_m, output_v, output_w, output_a = adam_step(
        clip * output_share,
        output_first,
        output_second,
        output_weight,
        output_average,
        1.0 / math.sqrt(max(1, V_ALL * 16 // LEN)),
    )
    gate_up_m, gate_up_v, gate_up_w, gate_up_a = adam_step(
        clip * gate_up_share,
        gate_up_first,
        gate_up_second,
        gate_up_weight,
        gate_up_average,
        1.0 / math.sqrt(D),
    )
    down_m, down_v, down_w, down_a = adam_step(
        clip * down_share, down_first, down_second, down_weight, down_average, 1.0 / math.sqrt(FF)
    )
    gains_m, gains_v, gains_w, gains_a = adam_step(
        clip * gains_share, gains_first, gains_second, gains, gains_average, 0.4
    )
    return (
        block_out,
        input_grad,
        grad_norm,
        qk_m,
        qk_v,
        qk_w,
        qk_a,
        value_m,
        value_v,
        value_w,
        value_a,
        output_m,
        output_v,
        output_w,
        output_a,
        gate_up_m,
        gate_up_v,
        gate_up_w,
        gate_up_a,
        down_m,
        down_v,
        down_w,
        down_a,
        gains_m,
        gains_v,
        gains_w,
        gains_a,
    )


def solution(mesh):
    placed = (
        P("dp", None),
        P("dp", None),
        P(None, "dp", None),
        P(None, "dp", None),
        P(None, "dp", None),
        P(None, "dp", None),
        P("dp", "mp"),
        P("dp", "mp"),
        P("dp", "mp"),
        P("dp", "mp"),
        P("mp", "dp"),
        P("mp", "dp"),
        P("mp", "dp"),
        P("mp", "dp"),
        P(None, "dp", "mp"),
        P(None, "dp", "mp"),
        P(None, "dp", "mp"),
        P(None, "dp", "mp"),
        P("mp", "dp"),
        P("mp", "dp"),
        P("mp", "dp"),
        P("mp", "dp"),
        P(None, "dp"),
        P(None, "dp"),
        P(None, "dp"),
        P(None, "dp"),
    )
    return jax.shard_map(
        on_device,
        mesh=mesh,
        in_specs=placed,
        out_specs=(
            P("dp", "mp"),
            P("dp", "mp"),
            P(),
            P(None, "dp", None),
            P(None, "dp", None),
            P(None, "dp", None),
            P(None, "dp", None),
            P("dp", "mp"),
            P("dp", "mp"),
            P("dp", "mp"),
            P("dp", "mp"),
            P("mp", "dp"),
            P("mp", "dp"),
            P("mp", "dp"),
            P("mp", "dp"),
            P(None, "dp", "mp"),
            P(None, "dp", "mp"),
            P(None, "dp", "mp"),
            P(None, "dp", "mp"),
            P("mp", "dp"),
            P("mp", "dp"),
            P("mp", "dp"),
            P("mp", "dp"),
            P(None, "dp"),
            P(None, "dp"),
            P(None, "dp"),
            P(None, "dp"),
        ),
        check_vma=False,
    )
```

profile of v0, /device:TPU:0, one launch (start us, length us, event | category | flops | bytes accessed | tf_op | source)
XLA Modules:
  0.0 1489.0 jit_solution(11503148982517520819)
XLA Ops:
  9.9 22.2 %all_gather.21 = bf16[2,1024]{1,0:T(2,128)(2,1)S(1)} all-gather(bf16[2,128]{1,0:T(2,128)(2,1)S(1)} %convert_element_type.163), channel_id=1, replica_groups=mesh['dp'=8,'mp'=4] {'dp'}, dimensions={1}, use_global_device_ids=true | all-gather | bytes 4608 | tf_op jit(solution)/shard_map/all_gather | solution.py:121
  32.2 5.1 fusion.56
  37.9 31.9 %all_gather.22 = bf16[1024,256]{1,0:T(8,128)(2,1)S(1)} all-gather(bf16[128,256]{1,0:T(8,128)(2,1)S(1)} %convert_element_type.165), channel_id=1, replica_groups=mesh['dp'=8,'mp'=4] {'dp'}, dimensions={0}, use_global_device_ids=true | all-gather | bytes 589824 | tf_op jit(solution)/shard_map/all_gather | solution.py:117
  80.9 5.6 copy.95
  86.5 28.1 %all_gather.24 = bf16[256,1024]{1,0:T(8,128)(2,1)} all-gather(bf16[256,128]{1,0:T(8,128)(2,1)S(1)} %convert_element_type.171), channel_id=1, replica_groups=mesh['dp'=8,'mp'=4] {'dp'}, dimensions={1}, use_global_device_ids=true | all-gather | bytes 589824 | tf_op jit(solution)/shard_map/all_gather | solution.py:118
  114.6 6.1 convolution_convert_fusion.3
  121.3 6.1 convolution_convert_fusion.4
  129.8 35.0 %while.30 = (s32[]{:T(128)}, f32[4,1024,4,64]{1,3,2,0:T(8,128)}, f32[4,1024,4]{1,2,0:T(4,128)S(1)}, bf16[4,1024,4,64]{1,3,2,0:T(8,128)(2,1)S(1)}, bf16[4,1024,4,...) while((s32[]{:T(128)}, f32[4,1024,4,64]{1,3,2,0:T(8,128)}, ...), condition=%wide.region_3.4_spmd, body=%wide.region_1.3_spmd.sunk | while | flops 706736128 | bytes 27052120 | solution.py:146
  130.5 5.6 fusion.150
  139.2 5.6 fusion.150
  147.9 5.6 fusion.150
  156.6 5.6 fusion.150
  164.8 4.0 divide_convert_fusion.3
  172.6 5.7 convolution_convert_fusion.1
  181.0 148.5 %all-reduce.3.cloned.1.call-done = bf16[4096,1024]{1,0:T(8,128)(2,1)} async-done(((bf16[4096,1024]{1,0:T(8,128)(2,1)}), bf16[4096,1024]{1,0:T(8,128)(2,1)}) %all-reduce.3.cloned.1.call-update) | async-done | bytes 8388624 | tf_op jit(solution)/shard_map/psum | solution.py:149
  329.6 8.6 multiply_reduce_fusion
  338.1 10.8 multiply_convert_fusion.9
  348.9 42.7 %all-gather.7.cloned.1.call-done = bf16[2,1024,688]{1,2,0:T(8,128)(2,1)} async-done(((bf16[2,128,688]{1,2,0:T(8,128)(2,1)}), bf16[2,1024,688]{1,2,0:T(8,128)(2,1)}) %all-gather.7.cloned.1.call-update) | async-done | bytes 2818064 | tf_op jit(solution)/shard_map/all_gather | solution.py:119
  391.6 12.5 fusion.68
  404.1 8.8 fusion.67
  412.9 22.6 %all-gather.9.cloned.1.call-done = bf16[688,1024]{1,0:T(8,128)(2,1)} async-done(((bf16[688,128]{1,0:T(8,128)(2,1)}), bf16[688,1024]{1,0:T(8,128)(2,1)}) %all-gather.9.cloned.1.call-update) | async-done | bytes 1409040 | tf_op jit(solution)/shard_map/all_gather | solution.py:120
  435.5 22.1 %multiply_convert_fusion.10 = (bf16[4096,688]{0,1:T(8,128)(2,1)}, bf16[4096,688]{0,1:T(8,128)(2,1)}, bf16[4096,688]{0,1:T(8,128)(2,1)}) fusion(f32[4096,688]{0,1:T(8,128)} %fusion.67, f32[4096,688]{0,1:T(8,128)} %fusion.68, bf16[4096,1024]{1,0:T(8,128)(2,1)} %param.31, bf16[688,1024]{1,0:T(8,128)(2,1)} %all-gather.9.cloned.1.call-done), kind=kOutput, calls=%fused_computation.84 | convolution fusion | flops 5816451072 | bytes 49250304 | tf_op jit(solution)/shard_map/dot_general | solution.py:24
  457.6 13.2 fusion.66
  470.8 12.5 add_convert_fusion
  483.4 151.4 %all-reduce.5.cloned.1.call-done = bf16[4096,1024]{1,0:T(8,128)(2,1)} async-done(((bf16[4096,1024]{1,0:T(8,128)(2,1)}), bf16[4096,1024]{1,0:T(8,128)(2,1)}) %all-reduce.5.cloned.1.call-update) | async-done | bytes 8388624 | tf_op jit(solution)/shard_map/psum | solution.py:170
  634.8 12.0 fusion.55
  646.8 17.5 %fusion.53 = (f32[4096,1024]{1,0:T(8,128)S(1)}, f32[4096,1024]{1,0:T(8,128)}) fusion(bf16[4096,1024]{1,0:T(8,128)(2,1)} %all-reduce.5.cloned.1.call-done, bf16[4096,1024]{1,0:T(8,128)(2,1)} %param.31, f32[4096]{0:T(1024)S(1)} %broadcast_multiply_fusion.1, f32[4096]{0:T(1024)S(1)} %get-tuple-element.439, f32[1024]{0:T(1024)S(1)} %bitcast.225, ...), kind=kLoop, calls=%fused_computation.71 | loop fusion | flops 46137344 | bytes 67162112 | tf_op jit(solution)/shard_map/sub | solution.py:178
  664.3 5.7 copy-done.5
  670.1 4.4 fusion.64
  674.4 6.0 reshape.148
  680.5 141.2 %while.31 = (s32[]{:T(128)}, bf16[4,1024,4,16]{1,3,2,0:T(8,128)(2,1)}, bf16[4,1024,4,16]{1,3,2,0:T(8,128)(2,1)}, bf16[4,1024,4,64]{1,3,2,0:T(8,128)(2,1)}, bf16[...) while((s32[]{:T(128)}, ...), condition=%wide.region_11.12_spmd, body=%wide.region_9.11_spmd.sunk | while | flops 1535123456 | bytes 167644336 | solution.py:185
  690.7 5.7 copy-done
  696.4 4.8 fusion.165
  701.1 8.3 multiply_convert_fusion.16
  725.8 5.7 copy-done
  731.5 4.7 fusion.165
  736.3 8.3 multiply_convert_fusion.16
  761.0 5.7 copy-done
  766.7 4.7 fusion.165
  771.4 8.3 multiply_convert_fusion.16
  796.2 5.7 copy-done
  801.9 4.7 fusion.165
  806.6 8.3 multiply_convert_fusion.16
  832.6 9.6 fusion.75
  842.3 9.3 fusion.74
  851.6 18.5 %fusion.51 = (f32[1024]{0:T(1024)S(1)}, f32[4096]{0:T(1024)S(1)}, f32[4096,1024]{1,0:T(8,128)}) fusion(bf16[4096,1024]{1,0:T(8,128)(2,1)S(1)} %bitcast.205, f32[4096]{0:T(1024)S(1)} %copy-done.29, f32[1024]{0:T(1024)S(1)} %bitcast.221, bf16[4096,256]{0,1:T(8,128)(2,1)S(1)} %bitcast.208, bf16[1024,256]{1,0:T(8,128)(2,1)} %copy-done.19, ...), kind=kOutput, calls=%fused_computation.69 | convolution fusion | flops 2185227264 | bytes 61382656 | tf_op jit(solution)/shard_map/dot_general | solution.py:24
  871.2 11.6 fusion.92
  882.9 9.2 fusion.62
  892.1 7.4 fusion.91
  902.5 10.3 convolution_bitcast_fusion
  912.8 10.1 convolution_bitcast_fusion.1
  926.0 11.8 convolution_convert_fusion
  938.5 12.5 fusion.59
  953.7 6.1 psum.30
  960.4 50.7 %reduce-scatter.21.cloned.1.call-done = f32[688,128]{1,0:T(8,128)} async-done(((f32[688,1024]{1,0:T(8,128)}), f32[688,128]{1,0:T(8,128)}) %reduce-scatter.21.cloned.1.call-update) | async-done | bytes 352272 | tf_op jit(solution)/shard_map/reduce_scatter | solution.py:213
  1012.9 64.5 %reduce-scatter.17.cloned.1.call-done = f32[256,128]{1,0:T(8,128)} async-done(((f32[256,1024]{1,0:T(8,128)}), f32[256,128]{1,0:T(8,128)}) %reduce-scatter.17.cloned.1.call-update) | async-done | bytes 131088 | tf_op jit(solution)/shard_map/reduce_scatter | solution.py:211
  1078.9 64.1 %reduce-scatter.15.cloned.1.call-done = f32[128,256]{1,0:T(8,128)} async-done(((f32[1024,256]{1,0:T(8,128)}), f32[128,256]{1,0:T(8,128)}) %reduce-scatter.15.cloned.1.call-update) | async-done | bytes 131088 | tf_op jit(solution)/shard_map/reduce_scatter | solution.py:210
  1145.9 69.1 %reduce-scatter.23.cloned.1.call-done = f32[2,128,256]{1,2,0:T(8,128)} async-done(((f32[2,1024,256]{1,2,0:T(8,128)}), f32[2,128,256]{1,2,0:T(8,128)}) %reduce-scatter.23.cloned.1.call-update) | async-done | bytes 262160 | tf_op jit(solution)/shard_map/reduce_scatter | solution.py:209
  1217.9 108.5 %reduce-scatter.19.cloned.1.call-done = f32[2,128,688]{1,2,0:T(8,128)} async-done(((f32[2,1024,688]{1,2,0:T(8,128)}), f32[2,128,688]{1,2,0:T(8,128)}) %reduce-scatter.19.cloned.1.call-update) | async-done | bytes 704528 | tf_op jit(solution)/shard_map/reduce_scatter | solution.py:212
  1329.7 40.8 %psum.31 = f32[]{:T(128)} all-reduce(f32[]{:T(128)S(6)} %add.280), channel_id=1, replica_groups=mesh['dp'=8,'mp'=4] {'dp','mp'}, use_global_device_ids=true, to_apply=%region_29.30 | all-reduce | flops 1 | bytes 8 | tf_op jit(solution)/shard_map/psum | solution.py:225
  1390.8 10.6 reduce-scatter.11.cloned.1.call-done
  1401.4 4.6 add_convert_fusion.1
  1406.0 69.6 %reduce-scatter.13.cloned.1.call-done = bf16[4096,256]{1,0:T(8,128)(2,1)} async-done(((bf16[4096,1024]{1,0:T(8,128)(2,1)}), bf16[4096,256]{1,0:T(8,128)(2,1)}) %reduce-scatter.13.cloned.1.call-update) | async-done | bytes 2097168 | tf_op jit(solution)/shard_map/reduce_scatter | solution.py:202
  1475.6 5.2 convert_add_fusion.1
  (230 shorter events, 151.4 us)
Async XLA Ops:
  7.2 30.7 %copy-start.24 = (f32[128,256]{1,0:T(8,128)S(1)}, f32[128,256]{1,0:T(8,128)}, u32[]{:S(2)}) copy-start(f32[128,256]{1,0:T(8,128)} %param.36) | copy-start | bytes 393220
  7.2 30.7 %copy-start.26 = (f32[256,128]{1,0:T(8,128)S(1)}, f32[256,128]{1,0:T(8,128)}, u32[]{:S(2)}) copy-start(f32[256,128]{1,0:T(8,128)} %param.40) | copy-start | bytes 393220
  7.2 107.4 %all-gather.5.cloned.1.call-start = ((), (), s32[]{:S(2)}) async-start(), calls=%async_computation.8 | async-start | bytes 1179648 | tf_op jit(solution)/shard_map/all_gather | solution.py:116
  9.0 320.6 %all-reduce.3.cloned.1.call-start = ((), (), s32[]{:S(2)}) async-start(), calls=%async_computation.9 | async-start | bytes 16777216 | tf_op jit(solution)/shard_map/psum | solution.py:149
  9.0 60.8 %copy-start.1 = (bf16[4096,1024]{1,0:T(8,128)(2,1)S(1)}, bf16[4096,1024]{1,0:T(8,128)(2,1)}, u32[]{:S(2)}) copy-start(bf16[4096,1024]{1,0:T(8,128)(2,1)} %param.30) | copy-start | bytes 25165828
  32.2 40.0 %copy-start.34 = (f32[1,1024]{1,0:T(1,128)}, f32[1,1024]{1,0:T(1,128)S(1)}, u32[]{:S(2)}) copy-start(f32[1,1024]{1,0:T(1,128)S(1)} %get-tuple-element.441) | copy-start | bytes 12292
  37.9 32.0 %copy-start.28 = (f32[4096]{0:T(1024)}, f32[4096]{0:T(1024)S(1)}, u32[]{:S(2)}) copy-start(f32[4096]{0:T(1024)S(1)} %get-tuple-element.438) | copy-start | bytes 49156
  69.9 2.3 copy-start.19
  72.1 3.2 copy-start.2
  164.8 6.5 copy-start.30
  164.8 13.5 copy-start.6
  164.8 13.5 copy-start.12
  164.8 13.5 copy-start.13
  164.8 7.8 copy-start.14
  171.3 1.3 copy-start.7
  178.3 2.0 copy-start.20
  178.3 1.2 copy-start.16
  178.3 213.3 %all-gather.7.cloned.1.call-start = ((), (), s32[]{:S(2)}) async-start(), calls=%async_computation.10 | async-start | bytes 3170304 | tf_op jit(solution)/shard_map/all_gather | solution.py:119
  180.2 255.3 %all-gather.9.cloned.1.call-start = ((), (), s32[]{:S(2)}) async-start(), calls=%async_computation.11 | async-start | bytes 1585152 | tf_op jit(solution)/shard_map/all_gather | solution.py:120
  181.0 453.8 %all-reduce.5.cloned.1.call-start = ((), (), s32[]{:S(2)}) async-start(), calls=%async_computation.13 | async-start | bytes 16777216 | tf_op jit(solution)/shard_map/psum | solution.py:170
  391.6 12.5 copy-start.10
  391.6 12.5 copy-start.40
  457.6 13.2 copy-start.42
  483.3 416.3 %all-gather.11.cloned.1.call-start = ((), (), s32[]{:S(2)}) async-start(), calls=%async_computation.19 | async-start | bytes 1310720 | tf_op jit(solution)/shard_map/all_gather | solution.py:205
  646.8 23.2 %copy-start.15 = (bf16[256,1024]{1,0:T(8,128)(2,1)S(1)}, bf16[256,1024]{1,0:T(8,128)(2,1)}, u32[]{:S(2)}) copy-start(bf16[256,1024]{1,0:T(8,128)(2,1)} %all_gather.24) | copy-start | bytes 1572868
  664.3 5.7 copy-start.5
  684.1 6.5 copy-start.4
  690.6 5.7 copy-start
  719.3 6.5 copy-start.4
  725.8 5.7 copy-start
  754.5 6.5 copy-start.4
  761.0 5.7 copy-start
  789.6 6.5 copy-start.4
  796.2 5.7 copy-start
  821.7 6.3 copy-start.3
  825.9 25.6 %copy-start.9 = (bf16[32,8,4,1024]{3,1,2,0:T(8,128)(2,1)}, bf16[32,8,4,1024]{3,1,2,0:T(8,128)(2,1)S(1)}, u32[]{:S(2)}) copy-start(bf16[32,8,4,1024]{3,1,2,0:T(8,128)(2,1)S(1)} %copy.128) | copy-start | bytes 6291460
  828.0 1.6 copy-start.27
  830.2 1.6 copy-start.11
  832.6 120.0 %reduce-scatter.25.cloned.1.call-start = ((), (), s32[]{:S(2)}) async-start(), calls=%async_computation.21 | async-start | bytes 589824
  832.6 18.9 %slice-start = ((s8[8388608]{0:T(1024)(128)(4,1)}), s8[4194304]{0:T(1024)(128)(4,1)S(1)}, s32[]{:S(2)}) async-start(s8[8388608]{0:T(1024)(128)(4,1)} %bitcast.204), calls=%async_computation.22 | async-start | bytes 8388608
  842.3 9.3 slice-start.1
  842.3 9.3 copy-start.29
  842.3 9.3 copy-start.35
  851.6 18.5 %copy-start.37 = (f32[1024]{0:T(1024)S(1)}, f32[1024]{0:T(1024)}, u32[]{:S(2)}) copy-start(f32[1024]{0:T(1024)} %get-tuple-element.368) | copy-start | bytes 12292
  871.1 140.0 %reduce-scatter.21.cloned.1.call-start = ((), (), s32[]{:S(2)}) async-start(), calls=%async_computation.18 | async-start | bytes 3170304 | tf_op jit(solution)/shard_map/reduce_scatter | solution.py:213
  871.2 11.7 copy-start.8
  882.9 194.5 %reduce-scatter.17.cloned.1.call-start = ((), (), s32[]{:S(2)}) async-start(), calls=%async_computation.16 | async-start | bytes 1179648 | tf_op jit(solution)/shard_map/reduce_scatter | solution.py:211
  892.1 250.9 %reduce-scatter.15.cloned.1.call-start = ((), (), s32[]{:S(2)}) async-start(), calls=%async_computation.15 | async-start | bytes 1179648 | tf_op jit(solution)/shard_map/reduce_scatter | solution.py:210
  899.6 315.4 %reduce-scatter.23.cloned.1.call-start = ((), (), s32[]{:S(2)}) async-start(), calls=%async_computation.20 | async-start | bytes 2359296 | tf_op jit(solution)/shard_map/reduce_scatter | solution.py:209
  902.5 423.9 %reduce-scatter.19.cloned.1.call-start = ((), (), s32[]{:S(2)}) async-start(), calls=%async_computation.17 | async-start | bytes 6340608 | tf_op jit(solution)/shard_map/reduce_scatter | solution.py:212
  922.9 3.1 copy-start.41
  926.0 475.4 %reduce-scatter.11.cloned.1.call-start = ((), (), s32[]{:S(2)}) async-start(), calls=%async_computation.12 | async-start | bytes 10485760 | tf_op jit(solution)/shard_map/reduce_scatter | solution.py:160
  937.8 537.8 %reduce-scatter.13.cloned.1.call-start = ((), (), s32[]{:S(2)}) async-start(), calls=%async_computation.14 | async-start | bytes 10485760 | tf_op jit(solution)/shard_map/reduce_scatter | solution.py:202
  951.0 0.9 copy-start.23
  951.0 1.1 copy-start.31
  951.0 1.2 copy-start.32
  951.0 1.4 copy-start.33
  951.0 429.8 %copy-start.25 = (f32[128,256]{1,0:T(8,128)S(1)}, f32[128,256]{1,0:T(8,128)}, u32[]{:S(2)}) copy-start(f32[128,256]{1,0:T(8,128)} %param.36) | copy-start | bytes 393220
  951.1 433.7 %copy-start.21 = (f32[688,128]{1,0:T(8,128)S(1)}, f32[688,128]{1,0:T(8,128)}, u32[]{:S(2)}) copy-start(f32[688,128]{1,0:T(8,128)} %param.48) | copy-start | bytes 1056772
  951.1 436.2 %copy-start.17 = (f32[2,128,688]{1,2,0:T(8,128)S(1)}, f32[2,128,688]{1,2,0:T(8,128)}, u32[]{:S(2)}) copy-start(f32[2,128,688]{1,2,0:T(8,128)} %param.44) | copy-start | bytes 2113540
  953.7 417.5 %copy-start.38 = (f32[1,128]{1,0:T(1,128)}, f32[1,128]{1,0:T(1,128)S(1)}, u32[]{:S(2)}) copy-start(f32[1,128]{1,0:T(1,128)S(1)} %copy.124) | copy-start | bytes 1540
  959.8 411.4 %copy-start.39 = (f32[1,128]{1,0:T(1,128)}, f32[1,128]{1,0:T(1,128)S(1)}, u32[]{:S(2)}) copy-start(f32[1,128]{1,0:T(1,128)S(1)} %psum.30) | copy-start | bytes 1540
  1011.1 373.6 %copy-start.22 = (f32[688,128]{1,0:T(8,128)S(1)}, f32[688,128]{1,0:T(8,128)}, u32[]{:S(2)}) copy-start(f32[688,128]{1,0:T(8,128)} %reduce-scatter.21.cloned.1.call-done) | copy-start | bytes 1056772
  1326.4 60.9 %copy-start.18 = (f32[2,128,688]{1,2,0:T(8,128)S(1)}, f32[2,128,688]{1,2,0:T(8,128)}, u32[]{:S(2)}) copy-start(f32[2,128,688]{1,2,0:T(8,128)} %reduce-scatter.19.cloned.1.call-done) | copy-start | bytes 2113540
  (1 other events, 0.7 us)
Sparse Core Ops, SparseCore 0:
  10.8 46.0 all-gather.4
  178.4 151.0 all-reduce.2
  332.2 59.3 all-gather.6
  394.1 41.3 all-gather.8
  483.5 151.3 all-reduce.4
  832.7 16.8 all-gather.10
  871.3 62.0 reduce-scatter.24
  937.9 73.2 reduce-scatter.20
  1014.9 62.3 reduce-scatter.16
  1080.6 62.3 reduce-scatter.14
  1147.6 67.3 reduce-scatter.22
  1218.9 107.4 reduce-scatter.18
  1329.2 72.2 reduce-scatter.10
  1403.8 71.7 reduce-scatter.12
where the time goes:
time: 1500 us; the launch traced here: 1490 us
  waiting for transfers between devices  802 us (53%)
  matrix products  319 us (21%)
  other arithmetic  131 us (9%)
  blocking collectives  129 us (9%)
  local copies, waits for them, and re-layouts  84.8 us (6%)
  between operations  20.9 us (1%)
    psum x1, waiting for transfers between devices, on_device(): lax.psum((against(grad_gate, gate_up_local[0]) + against(grad_lift, gate_...  151 us
    psum x1, waiting for transfers between devices, on_device(): lax.psum(attn_part.astype(jnp.bfloat16), 'mp').astype(jnp.float32)  149 us
    reduce_scatter x1, waiting for transfers between devices, on_device(): lax.psum_scatter(gate_up_grad, 'dp', scatter_dimension=1, tiled=True)  108 us
    dot_general x7, matrix products, against(): lax.dot_general(left, right, (((1,), (1,)), ((), ())), preferred_element_...  89.6 us
    reduce_scatter x1, waiting for transfers between devices, on_device(): lax.psum_scatter(input_part.astype(jnp.bfloat16), 'mp', scatter_dimension...  69.6 us
    reduce_scatter x1, waiting for transfers between devices, on_device(): lax.psum_scatter(qk_grad, 'dp', scatter_dimension=1, tiled=True)  69.1 us
    reduce_scatter x1, waiting for transfers between devices, on_device(): lax.psum_scatter(output_grad, 'dp', scatter_dimension=1, tiled=True)  64.5 us
    reduce_scatter x1, waiting for transfers between devices, on_device(): lax.psum_scatter(value_grad, 'dp', scatter_dimension=0, tiled=True)  64.1 us
  transfers between devices with their start and end apart: 14, of which 11 were waited for; matrix products, arithmetic and copies ran while one was open for 14% of the time, Pallas kernels for 0%

commit v1 on v0

--- a/solution.py
+++ b/solution.py
@@ -1,3 +1,4 @@
+import functools
 import math
 import jax
 import jax.numpy as jnp
@@ -12,6 +13,26 @@
 V_ALL = 1024
 LEN = 1024
 STEP = 5
+
+
+def supply_all_packet_for(u, net_axis):
+    n_chips = lax.axis_size(net_axis)
+    arrivals = [(jj, (jj + 1) % n_chips) for jj in range(n_chips)]
+    kept_rows = [(jj, (jj - 1) % n_chips) for jj in range(n_chips)]
+    seen_now, known = ([u], [u])
+    for _ in range(n_chips // 2):
+        seen_now.append(lax.ppermute(seen_now[-1], net_axis, arrivals))
+    for _ in range((n_chips - 1) // 2):
+        known.append(lax.ppermute(known[-1], net_axis, kept_rows))
+    lower = jnp.roll(
+        jnp.concatenate([*seen_now[::-1], *known[1:]], 1),
+        (lax.axis_index(net_axis) - n_chips // 2) * u.shape[1],
+        1,
+    )
+    return lower
+
+
+guide_the_object = functools.partial(supply_all_packet_for, net_axis="dp")
 
 
 def inner(left, right):
@@ -116,7 +137,7 @@
         lax.all_gather(qk_weight.astype(jnp.bfloat16), "dp", axis=1, tiled=True),
         lax.all_gather(value_weight.astype(jnp.bfloat16), "dp", axis=0, tiled=True),
         lax.all_gather(output_weight.astype(jnp.bfloat16), "dp", axis=1, tiled=True),
-        lax.all_gather(gate_up_weight.astype(jnp.bfloat16), "dp", axis=1, tiled=True),
+        guide_the_object(gate_up_weight.astype(jnp.bfloat16)),
         lax.all_gather(down_weight.astype(jnp.bfloat16), "dp", axis=1, tiled=True),
         lax.all_gather(gains.astype(jnp.bfloat16), "dp", axis=1, tiled=True),
     )

time: 1500 us -> 1450 us (0.967)
  waiting for transfers between devices: 802 us -> 708 us
  local copies, waits for them, and re-layouts: 84.8 us -> 104 us
    all_gather x1 -> x0, waiting for transfers between devices: 42.7 us -> none  [on_device(): lax.all_gather(gate_up_weight.astype(jnp.bfloat16), 'dp', axis=1, tiled=T...]
    psum x1, waiting for transfers between devices: 149 us -> 119 us  [on_device(): lax.psum(attn_part.astype(jnp.bfloat16), 'mp').astype(jnp.float32)]
    all_gather x1, waiting for transfers between devices: 22.6 us -> 0.01 us  [on_device(): lax.all_gather(down_weight.astype(jnp.bfloat16), 'dp', axis=1, tiled=True)]
    unnamed x101 -> x116, local copies, waits for them, and re-layouts: 22.9 us -> 38.4 us
  transfers between devices with their start and end apart: 14 -> 20, of which waited for: 11 -> 9; matrix products, arithmetic and copies ran while one was open for 14% -> 19% of each run, Pallas kernels for 0% -> 0%
where the time goes in v1:
time: 1450 us; the launch traced here: 1440 us
  waiting for transfers between devices  708 us (49%)
  matrix products  319 us (22%)
  blocking collectives  143 us (10%)
  other arithmetic  131 us (9%)
  local copies, waits for them, and re-layouts  104 us (7%)
  between operations  21 us (1%)
    psum x1, waiting for transfers between devices, on_device(): lax.psum((against(grad_gate, gate_up_local[0]) + against(grad_lift, gate_...  153 us
    psum x1, waiting for transfers between devices, on_device(): lax.psum(attn_part.astype(jnp.bfloat16), 'mp').astype(jnp.float32)  119 us
    reduce_scatter x1, waiting for transfers between devices, on_device(): lax.psum_scatter(gate_up_grad, 'dp', scatter_dimension=1, tiled=True)  109 us
    dot_general x7, matrix products, against(): lax.dot_general(left, right, (((1,), (1,)), ((), ())), preferred_element_...  79 us
    reduce_scatter x1, waiting for transfers between devices, on_device(): lax.psum_scatter(input_part.astype(jnp.bfloat16), 'mp', scatter_dimension...  69.7 us
    reduce_scatter x1, waiting for transfers between devices, on_device(): lax.psum_scatter(qk_grad, 'dp', scatter_dimension=1, tiled=True)  68.7 us
    reduce_scatter x1, waiting for transfers between devices, on_device(): lax.psum_scatter(output_grad, 'dp', scatter_dimension=1, tiled=True)  64.7 us
    reduce_scatter x1, waiting for transfers between devices, on_device(): lax.psum_scatter(value_grad, 'dp', scatter_dimension=0, tiled=True)  64.3 us
  transfers between devices with their start and end apart: 20, of which 9 were waited for; matrix products, arithmetic and copies ran while one was open for 19% of the time, Pallas kernels for 0%

profile of v1, /device:TPU:0, one launch (start us, length us, event | category | flops | bytes accessed | tf_op | source)
XLA Modules:
  0.0 1439.5 jit_solution(2565225556244591234)
XLA Ops:
  10.1 6.0 collective-permute-start.4
  18.7 25.9 %all_gather.18 = bf16[2,1024]{1,0:T(2,128)(2,1)S(1)} all-gather(bf16[2,128]{1,0:T(2,128)(2,1)S(1)} %convert_element_type.163), channel_id=1, replica_groups=mesh['dp'=8,'mp'=4] {'dp'}, dimensions={1}, use_global_device_ids=true | all-gather | bytes 4608 | tf_op jit(solution)/shard_map/all_gather | solution.py:142
  44.7 5.1 fusion.56
  52.8 37.8 %all_gather.19 = bf16[1024,256]{1,0:T(8,128)(2,1)S(1)} all-gather(bf16[128,256]{1,0:T(8,128)(2,1)S(1)} %convert_element_type.165), channel_id=1, replica_groups=mesh['dp'=8,'mp'=4] {'dp'}, dimensions={0}, use_global_device_ids=true | all-gather | bytes 589824 | tf_op jit(solution)/shard_map/all_gather | solution.py:138
  96.3 5.6 copy.95
  101.9 32.4 %all_gather.21 = bf16[256,1024]{1,0:T(8,128)(2,1)} all-gather(bf16[256,128]{1,0:T(8,128)(2,1)S(1)} %convert_element_type.171), channel_id=1, replica_groups=mesh['dp'=8,'mp'=4] {'dp'}, dimensions={1}, use_global_device_ids=true | all-gather | bytes 589824 | tf_op jit(solution)/shard_map/all_gather | solution.py:139
  136.3 6.1 convolution_convert_fusion.3
  143.0 6.1 convolution_convert_fusion.4
  151.5 37.4 %while.30 = (s32[]{:T(128)}, f32[4,1024,4,64]{1,3,2,0:T(8,128)}, f32[4,1024,4]{1,2,0:T(4,128)}, bf16[4,1024,4,64]{1,3,2,0:T(8,128)(2,1)S(1)}, bf16[4,1024,4,16]{...) while((s32[]{:T(128)}, f32[4,1024,4,64]{1,3,2,0:T(8,128)}, ...), condition=%wide.region_3.4_spmd, body=%wide.region_1.3_spmd.sunk | while | flops 706736128 | bytes 27052120 | solution.py:167
  152.2 5.6 fusion.155
  161.5 5.6 fusion.155
  170.8 5.6 fusion.155
  180.1 5.6 fusion.155
  188.9 4.0 divide_convert_fusion.3
  196.7 5.6 convolution_convert_fusion.1
  202.4 4.5 collective-permute-start.6
  225.9 11.8 fusion.95
  237.7 118.8 %all-reduce.3.cloned.1.call-done = bf16[4096,1024]{1,0:T(8,128)(2,1)} async-done(((bf16[4096,1024]{1,0:T(8,128)(2,1)}), bf16[4096,1024]{1,0:T(8,128)(2,1)}) %all-reduce.3.cloned.1.call-update) | async-done | bytes 8388624 | tf_op jit(solution)/shard_map/psum | solution.py:170
  356.6 8.6 multiply_reduce_fusion
  365.1 7.5 multiply_convert_fusion.9
  375.9 10.0 fusion.68
  386.0 21.7 %multiply_convert_fusion.11 = (bf16[4096,688]{0,1:T(8,128)(2,1)}, bf16[4096,688]{0,1:T(8,128)(2,1)}, bf16[4096,688]{0,1:T(8,128)(2,1)}) fusion(f32[4096,688]{0,1:T(8,128)} %fusion.95, f32[4096,688]{0,1:T(8,128)} %fusion.68, bf16[4096,1024]{1,0:T(8,128)(2,1)} %copy-done.12, bf16[2,2048,688]{1,2,0:T(8,128)(2,1)} %constant_dynamic-update-slice_fusion, ...), kind=kOutput, calls=%fused_computation.85 | convolution fusion | flops 5816451072 | bytes 49250308 | tf_op jit(solution)/shard_map/dot_general | solution.py:174
  407.6 12.6 fusion.67
  420.2 12.8 add_convert_fusion
  433.1 153.1 %all-reduce.5.cloned.1.call-done = bf16[4096,1024]{1,0:T(8,128)(2,1)} async-done(((bf16[4096,1024]{1,0:T(8,128)(2,1)}), bf16[4096,1024]{1,0:T(8,128)(2,1)}) %all-reduce.5.cloned.1.call-update) | async-done | bytes 8388624 | tf_op jit(solution)/shard_map/psum | solution.py:191
  586.2 12.4 fusion.55
  598.6 17.5 %fusion.53 = (f32[4096,1024]{1,0:T(8,128)S(1)}, f32[4096,1024]{1,0:T(8,128)}) fusion(bf16[4096,1024]{1,0:T(8,128)(2,1)} %all-reduce.5.cloned.1.call-done, bf16[4096,1024]{1,0:T(8,128)(2,1)} %param.31, f32[4096]{0:T(1024)S(1)} %broadcast_multiply_fusion.1, f32[4096]{0:T(1024)S(1)} %get-tuple-element.439, f32[1024]{0:T(1024)S(1)} %bitcast.227, ...), kind=kLoop, calls=%fused_computation.71 | loop fusion | flops 46137344 | bytes 67162112 | tf_op jit(solution)/shard_map/sub | solution.py:199
  616.1 5.7 copy-done.5
  621.8 4.4 fusion.64
  626.2 6.0 reshape.148
  632.2 140.9 %while.31 = (s32[]{:T(128)}, bf16[4,1024,4,16]{1,3,2,0:T(8,128)(2,1)}, bf16[4,1024,4,16]{1,3,2,0:T(8,128)(2,1)}, bf16[4,1024,4,64]{1,3,2,0:T(8,128)(2,1)}, bf16[...) while((s32[]{:T(128)}, ...), condition=%wide.region_11.12_spmd, body=%wide.region_9.11_spmd.sunk | while | flops 1535123456 | bytes 167644336 | solution.py:206
  642.0 5.7 copy-done
  647.7 4.8 fusion.170
  652.5 8.3 multiply_convert_fusion.16
  677.2 5.7 copy-done
  682.9 4.7 fusion.170
  687.7 8.3 multiply_convert_fusion.16
  712.4 5.7 copy-done
  718.1 4.7 fusion.170
  722.8 8.3 multiply_convert_fusion.16
  747.6 5.7 copy-done
  753.3 4.7 fusion.170
  758.0 8.3 multiply_convert_fusion.16
  784.0 9.6 fusion.75
  793.7 9.3 fusion.74
  803.0 18.5 %fusion.51 = (f32[1024]{0:T(1024)S(1)}, f32[4096]{0:T(1024)S(1)}, f32[4096,1024]{1,0:T(8,128)}) fusion(bf16[4096,1024]{1,0:T(8,128)(2,1)S(1)} %bitcast.207, f32[4096]{0:T(1024)S(1)} %copy-done.32, f32[1024]{0:T(1024)S(1)} %bitcast.223, bf16[4096,256]{0,1:T(8,128)(2,1)S(1)} %bitcast.210, bf16[1024,256]{1,0:T(8,128)(2,1)} %copy-done.19, ...), kind=kOutput, calls=%fused_computation.69 | convolution fusion | flops 2185227264 | bytes 61382656 | tf_op jit(solution)/shard_map/dot_general | solution.py:45
  822.6 11.6 fusion.97
  834.4 9.1 fusion.62
  843.6 7.4 fusion.96
  853.9 10.3 convolution_bitcast_fusion.1
  864.3 10.1 convolution_bitcast_fusion
  877.4 11.8 convolution_convert_fusion
  890.0 12.5 fusion.59
  905.1 6.1 psum.30
  911.9 49.7 %reduce-scatter.21.cloned.1.call-done = f32[688,128]{1,0:T(8,128)} async-done(((f32[688,1024]{1,0:T(8,128)}), f32[688,128]{1,0:T(8,128)}) %reduce-scatter.21.cloned.1.call-update) | async-done | bytes 352272 | tf_op jit(solution)/shard_map/reduce_scatter | solution.py:234
  963.3 64.7 %reduce-scatter.17.cloned.1.call-done = f32[256,128]{1,0:T(8,128)} async-done(((f32[256,1024]{1,0:T(8,128)}), f32[256,128]{1,0:T(8,128)}) %reduce-scatter.17.cloned.1.call-update) | async-done | bytes 131088 | tf_op jit(solution)/shard_map/reduce_scatter | solution.py:232
  1029.5 64.3 %reduce-scatter.15.cloned.1.call-done = f32[128,256]{1,0:T(8,128)} async-done(((f32[1024,256]{1,0:T(8,128)}), f32[128,256]{1,0:T(8,128)}) %reduce-scatter.15.cloned.1.call-update) | async-done | bytes 131088 | tf_op jit(solution)/shard_map/reduce_scatter | solution.py:231
  1096.7 68.7 %reduce-scatter.23.cloned.1.call-done = f32[2,128,256]{1,2,0:T(8,128)} async-done(((f32[2,1024,256]{1,2,0:T(8,128)}), f32[2,128,256]{1,2,0:T(8,128)}) %reduce-scatter.23.cloned.1.call-update) | async-done | bytes 262160 | tf_op jit(solution)/shard_map/reduce_scatter | solution.py:230
  1168.3 108.7 %reduce-scatter.19.cloned.1.call-done = f32[2,128,688]{1,2,0:T(8,128)} async-done(((f32[2,1024,688]{1,2,0:T(8,128)}), f32[2,128,688]{1,2,0:T(8,128)}) %reduce-scatter.19.cloned.1.call-update) | async-done | bytes 704528 | tf_op jit(solution)/shard_map/reduce_scatter | solution.py:233
  1280.2 40.8 %psum.31 = f32[]{:T(128)} all-reduce(f32[]{:T(128)S(6)} %add.293), channel_id=1, replica_groups=mesh['dp'=8,'mp'=4] {'dp','mp'}, use_global_device_ids=true, to_apply=%region_29.30 | all-reduce | flops 1 | bytes 8 | tf_op jit(solution)/shard_map/psum | solution.py:246
  1341.3 10.5 reduce-scatter.11.cloned.1.call-done
  1351.8 4.6 add_convert_fusion.1
  1356.4 69.7 %reduce-scatter.13.cloned.1.call-done = bf16[4096,256]{1,0:T(8,128)(2,1)} async-done(((bf16[4096,1024]{1,0:T(8,128)(2,1)}), bf16[4096,256]{1,0:T(8,128)(2,1)}) %reduce-scatter.13.cloned.1.call-update) | async-done | bytes 2097168 | tf_op jit(solution)/shard_map/reduce_scatter | solution.py:223
  1426.1 5.2 convert_add_fusion.1
  (259 shorter events, 175.2 us)
Async XLA Ops:
  7.2 129.1 %all-gather.4.cloned.1.call-start = ((), (), s32[]{:S(2)}) async-start(), calls=%async_computation.8 | async-start | bytes 1179648 | tf_op jit(solution)/shard_map/all_gather | solution.py:137
  8.9 217.0 %all-gather.6.cloned.1.call-start = ((), (), s32[]{:S(2)}) async-start(), calls=%async_computation.10 | async-start | bytes 1585152 | tf_op jit(solution)/shard_map/all_gather | solution.py:141
  10.1 124.2 %collective-permute-start.4 = (bf16[2,128,688]{1,2,0:T(8,128)(2,1)S(1)}, bf16[2,128,688]{1,2,0:T(8,128)(2,1)S(1)}, u32[]{:S(2)}, u32[]{:S(2)}) collective-permute-start(bf16[2,128,688]{1,2,0:T(8,128)(2,1)S(1)} %convert_element_type.175), channel_id=1, source_target_pairs={{0,28},{4,0},{8,4},{12,8},{16,12},{20,16},{24,20},{28,24},{1,29},{... | collective-permute-start | bytes 1056776 | tf_op jit(solution)/shard_map/ppermute | solution.py:26
  16.1 34.3 %collective-permute-start = (bf16[2,128,688]{1,2,0:T(8,128)(2,1)S(1)}, bf16[2,128,688]{1,2,0:T(8,128)(2,1)S(1)}, u32[]{:S(2)}, u32[]{:S(2)}) collective-permute-start(bf16[2,128,688]{1,2,0:T(8,128)(2,1)S(1)} %convert_element_type.175), channel_id=1, source_target_pairs={{0,4},{4,8},{8,12},{12,16},{16,20},{20,24},{24,28},{28,0},{1,5},{5... | collective-permute-start | bytes 1056776 | tf_op jit(solution)/shard_map/ppermute | solution.py:24
  17.8 338.7 %all-reduce.3.cloned.1.call-start = ((), (), s32[]{:S(2)}) async-start(), calls=%async_computation.9 | async-start | bytes 16777216 | tf_op jit(solution)/shard_map/psum | solution.py:170
  17.9 32.6 %copy-start.1 = (bf16[4096,1024]{1,0:T(8,128)(2,1)S(1)}, bf16[4096,1024]{1,0:T(8,128)(2,1)}, u32[]{:S(2)}) copy-start(bf16[4096,1024]{1,0:T(8,128)(2,1)} %param.30) | copy-start | bytes 25165828
  50.4 2.3 copy-start.31
  50.4 2.3 copy-start.20
  50.4 40.1 %collective-permute-start.1 = (bf16[2,128,688]{1,2,0:T(8,128)(2,1)S(1)}, bf16[2,128,688]{1,2,0:T(8,128)(2,1)S(1)}, u32[]{:S(2)}, u32[]{:S(2)}) collective-permute-start(bf16[2,128,688]{1,2,0:T(8,128)(2,1)S(1)} %collective-permute-done), channel_id=1, source_target_pairs={{0,4},{4,8},{8,12},{12,16},{16,20},{20,24},{24,28},{28,0},{1,5},{5... | collective-permute-start | bytes 1056776 | tf_op jit(solution)/shard_map/ppermute | solution.py:24
  50.5 2.3 copy-start.27
  52.8 40.2 %copy-start.2 = (bf16[4096,1024]{1,0:T(8,128)(2,1)}, bf16[4096,1024]{1,0:T(8,128)(2,1)S(1)}, u32[]{:S(2)}) copy-start(bf16[4096,1024]{1,0:T(8,128)(2,1)S(1)} %fusion.50) | copy-start | bytes 25165828
  90.5 2.4 copy-start.19
  90.6 2.5 copy-start.29
  90.6 2.4 copy-start.22
  90.6 45.5 %collective-permute-start.2 = (bf16[2,128,688]{1,2,0:T(8,128)(2,1)S(1)}, bf16[2,128,688]{1,2,0:T(8,128)(2,1)}, u32[]{:S(2)}, u32[]{:S(2)}) collective-permute-start(bf16[2,128,688]{1,2,0:T(8,128)(2,1)S(1)} %collective-permute-done.1), channel_id=1, source_target_pairs={{0,4},{4,8},{8,12},{12,16},{16,20},{20,24},{24,28},{28,0},{1,5},{5... | collective-permute-start | bytes 1056776 | tf_op jit(solution)/shard_map/ppermute | solution.py:24
  134.3 68.1 %collective-permute-start.5 = (bf16[2,128,688]{1,2,0:T(8,128)(2,1)S(1)}, bf16[2,128,688]{1,2,0:T(8,128)(2,1)}, u32[]{:S(2)}, u32[]{:S(2)}) collective-permute-start(bf16[2,128,688]{1,2,0:T(8,128)(2,1)S(1)} %collective-permute-done.4), channel_id=1, source_target_pairs={{0,28},{4,0},{8,4},{12,8},{16,12},{20,16},{24,20},{28,24},{1,29},{... | collective-permute-start | bytes 1056776 | tf_op jit(solution)/shard_map/ppermute | solution.py:26
  136.0 70.9 %collective-permute-start.3 = (bf16[2,128,688]{1,2,0:T(8,128)(2,1)}, bf16[2,128,688]{1,2,0:T(8,128)(2,1)}, u32[]{:S(2)}, u32[]{:S(2)}) collective-permute-start(bf16[2,128,688]{1,2,0:T(8,128)(2,1)} %collective-permute-done.2), channel_id=1, source_target_pairs={{0,4},{4,8},{8,12},{12,16},{16,20},{20,24},{24,28},{28,0},{1,5},{5... | collective-permute-start | bytes 1056776 | tf_op jit(solution)/shard_map/ppermute | solution.py:24
  188.9 6.5 copy-start.14
  188.9 6.5 copy-start.15
  188.9 13.4 copy-start.6
  188.9 7.8 copy-start.16
  202.3 10.0 copy-start.10
  202.3 8.3 copy-start.23
  202.3 9.2 copy-start.21
  202.3 383.9 %all-reduce.5.cloned.1.call-start = ((), (), s32[]{:S(2)}) async-start(), calls=%async_computation.12 | async-start | bytes 16777216 | tf_op jit(solution)/shard_map/psum | solution.py:191
  202.4 13.2 collective-permute-start.6
  372.6 3.3 copy-start.12
  407.6 12.6 copy-start.43
  433.1 418.0 %all-gather.8.cloned.1.call-start = ((), (), s32[]{:S(2)}) async-start(), calls=%async_computation.18 | async-start | bytes 1310720 | tf_op jit(solution)/shard_map/all_gather | solution.py:226
  598.6 23.2 %copy-start.17 = (bf16[256,1024]{1,0:T(8,128)(2,1)S(1)}, bf16[256,1024]{1,0:T(8,128)(2,1)}, u32[]{:S(2)}) copy-start(bf16[256,1024]{1,0:T(8,128)(2,1)} %all_gather.21) | copy-start | bytes 1572868
  616.1 5.7 copy-start.5
  635.5 6.5 copy-start.4
  642.0 5.7 copy-start
  670.7 6.5 copy-start.4
  677.2 5.7 copy-start
  705.9 6.5 copy-start.4
  712.4 5.7 copy-start
  741.0 6.5 copy-start.4
  747.5 5.7 copy-start
  773.1 6.3 copy-start.3
  777.4 25.6 %copy-start.9 = (bf16[32,8,4,1024]{3,1,2,0:T(8,128)(2,1)}, bf16[32,8,4,1024]{3,1,2,0:T(8,128)(2,1)S(1)}, u32[]{:S(2)}) copy-start(bf16[32,8,4,1024]{3,1,2,0:T(8,128)(2,1)S(1)} %copy.128) | copy-start | bytes 6291460
  779.4 1.6 copy-start.30
  784.0 120.0 %reduce-scatter.25.cloned.1.call-start = ((), (), s32[]{:S(2)}) async-start(), calls=%async_computation.20 | async-start | bytes 589824
  784.0 19.0 %slice-start = ((s8[8388608]{0:T(1024)(128)(4,1)}), s8[4194304]{0:T(1024)(128)(4,1)S(1)}, s32[]{:S(2)}) async-start(s8[8388608]{0:T(1024)(128)(4,1)} %bitcast.206), calls=%async_computation.21 | async-start | bytes 8388608
  793.7 9.3 slice-start.1
  793.7 9.3 copy-start.32
  793.7 9.3 copy-start.37
  803.0 18.5 %copy-start.39 = (f32[1024]{0:T(1024)S(1)}, f32[1024]{0:T(1024)}, u32[]{:S(2)}) copy-start(f32[1024]{0:T(1024)} %get-tuple-element.368) | copy-start | bytes 12292
  822.6 139.0 %reduce-scatter.21.cloned.1.call-start = ((), (), s32[]{:S(2)}) async-start(), calls=%async_computation.17 | async-start | bytes 3170304 | tf_op jit(solution)/shard_map/reduce_scatter | solution.py:234
  822.6 11.7 copy-start.8
  834.3 193.7 %reduce-scatter.17.cloned.1.call-start = ((), (), s32[]{:S(2)}) async-start(), calls=%async_computation.15 | async-start | bytes 1179648 | tf_op jit(solution)/shard_map/reduce_scatter | solution.py:232
  843.5 250.3 %reduce-scatter.15.cloned.1.call-start = ((), (), s32[]{:S(2)}) async-start(), calls=%async_computation.14 | async-start | bytes 1179648 | tf_op jit(solution)/shard_map/reduce_scatter | solution.py:231
  851.0 314.3 %reduce-scatter.23.cloned.1.call-start = ((), (), s32[]{:S(2)}) async-start(), calls=%async_computation.19 | async-start | bytes 2359296 | tf_op jit(solution)/shard_map/reduce_scatter | solution.py:230
  853.9 423.1 %reduce-scatter.19.cloned.1.call-start = ((), (), s32[]{:S(2)}) async-start(), calls=%async_computation.16 | async-start | bytes 6340608 | tf_op jit(solution)/shard_map/reduce_scatter | solution.py:233
  874.4 3.1 copy-start.42
  877.4 474.4 %reduce-scatter.11.cloned.1.call-start = ((), (), s32[]{:S(2)}) async-start(), calls=%async_computation.11 | async-start | bytes 10485760 | tf_op jit(solution)/shard_map/reduce_scatter | solution.py:181
  889.3 536.9 %reduce-scatter.13.cloned.1.call-start = ((), (), s32[]{:S(2)}) async-start(), calls=%async_computation.13 | async-start | bytes 10485760 | tf_op jit(solution)/shard_map/reduce_scatter | solution.py:223
  902.5 428.9 %copy-start.28 = (f32[128,256]{1,0:T(8,128)S(1)}, f32[128,256]{1,0:T(8,128)}, u32[]{:S(2)}) copy-start(f32[128,256]{1,0:T(8,128)} %param.36) | copy-start | bytes 393220
  902.5 432.8 %copy-start.24 = (f32[688,128]{1,0:T(8,128)S(1)}, f32[688,128]{1,0:T(8,128)}, u32[]{:S(2)}) copy-start(f32[688,128]{1,0:T(8,128)} %param.48) | copy-start | bytes 1056772
  902.5 435.3 %copy-start.11 = (f32[2,128,688]{1,2,0:T(8,128)S(1)}, f32[2,128,688]{1,2,0:T(8,128)}, u32[]{:S(2)}) copy-start(f32[2,128,688]{1,2,0:T(8,128)} %param.44) | copy-start | bytes 2113540
  905.1 416.6 %copy-start.40 = (f32[1,128]{1,0:T(1,128)}, f32[1,128]{1,0:T(1,128)S(1)}, u32[]{:S(2)}) copy-start(f32[1,128]{1,0:T(1,128)S(1)} %copy.124) | copy-start | bytes 1540
  911.3 410.5 %copy-start.41 = (f32[1,128]{1,0:T(1,128)}, f32[1,128]{1,0:T(1,128)S(1)}, u32[]{:S(2)}) copy-start(f32[1,128]{1,0:T(1,128)S(1)} %psum.30) | copy-start | bytes 1540
  961.6 373.7 %copy-start.25 = (f32[688,128]{1,0:T(8,128)S(1)}, f32[688,128]{1,0:T(8,128)}, u32[]{:S(2)}) copy-start(f32[688,128]{1,0:T(8,128)} %reduce-scatter.21.cloned.1.call-done) | copy-start | bytes 1056772
  1276.9 60.9 %copy-start.18 = (f32[2,128,688]{1,2,0:T(8,128)S(1)}, f32[2,128,688]{1,2,0:T(8,128)}, u32[]{:S(2)}) copy-start(f32[2,128,688]{1,2,0:T(8,128)} %reduce-scatter.19.cloned.1.call-done) | copy-start | bytes 2113540
  (8 other events, 8.9 us)
Sparse Core Ops, SparseCore 0:
  10.8 47.1 all-gather.3
  60.6 48.7 all-gather.5
  202.4 154.0 all-reduce.2
  433.2 153.0 all-reduce.4
  784.1 16.8 all-gather.7
  822.7 62.0 reduce-scatter.24
  889.3 72.2 reduce-scatter.20
  965.4 62.5 reduce-scatter.16
  1031.4 62.3 reduce-scatter.14
  1098.2 67.0 reduce-scatter.22
  1169.4 107.4 reduce-scatter.18
  1279.6 72.1 reduce-scatter.10
  1354.3 71.7 reduce-scatter.12
